TPU v7x, 128 devices: a whole 4x4x4 slice. The times are simulated.
128 devices in a mesh: layer: 8 (over z, y_lo), blk: 16 (over x, y_hi, core).
Axes of the slice: x: 4, y: 4 (y_hi: 2, y_lo: 2; y = y_hi * 2 + y_lo), z: 4, core: 2. Of those that a mesh axis runs over, the one named last changes fastest.
Arguments:
- iterate: bfloat16 [8, 1536, 12288], P('layer', 'blk'), may hold values from -0.0546875 to 0.0546875
Outputs:
- update: bfloat16 [8, 1536, 12288], P(None, 'blk', 'layer')
All inputs are finite; a program needn't handle non-finite values.
Results may differ from a plain program's by a relative error of at most 0.0095.
Values may be sent and summed in bfloat16 or wider, within the bound.
No kernel may reach another device: no remote copies, remote signals or barrier semaphores. Data moves between devices by JAX's collectives and lax.ppermute only.
A program may use at most 128 MiB of HBM per device.

v0:
```python
import math
import jax
import jax.numpy as jnp
from jax import lax
from jax.sharding import PartitionSpec as P

coeff_a = 3.4445
coeff_b = -4.775
coeff_c = 2.0315


def shards(iterate):
    local_rows = iterate.shape[1]
    width = iterate.shape[2]
    all_rows = local_rows * lax.axis_size("blk")
    scale = math.sqrt(max(all_rows, width))
    pieces = lax.all_gather(iterate, "blk", axis=1, tiled=True)
    gathered = pieces
    gram_tile = jnp.einsum("lrc,lkc->lrk", iterate, pieces, preferred_element_type=jnp.float32)
    gram_block = gram_tile
    gathered, gram_block = (gathered, gram_block)
    gram_half = gram_block.astype(jnp.bfloat16)
    square = jnp.einsum(
        "lrk,lkm->lrm",
        gram_half,
        lax.all_gather(gram_half, "blk", axis=1, tiled=True),
        preferred_element_type=jnp.float32,
    )
    mixing = (coeff_b * gram_half.astype(jnp.float32) + coeff_c * square).astype(jnp.bfloat16)
    result = coeff_a * iterate.astype(jnp.float32) + jnp.einsum(
        "lrk,lkc->lrc", mixing, gathered, preferred_element_type=jnp.float32
    )
    scaled_rows = (scale * result).astype(jnp.bfloat16)
    return lax.all_to_all(scaled_rows, "layer", split_axis=2, concat_axis=0, tiled=True)


def solution(mesh):
    return jax.shard_map(
        shards,
        mesh=mesh,
        in_specs=(P("layer", "blk", None),),
        out_specs=P(None, "blk", "layer"),
        check_vma=False,
    )
```

profile of v0, /device:TPU:0, one launch (start us, length us, event | category | flops | bytes accessed | tf_op | source)
XLA Modules:
  0.0 465.5 jit_solution(16663097031767835544)
XLA Ops:
  6.5 0.0 all-gather.4.cloned.1.call-start
  6.5 0.7 all-gather.4.cloned.1.call-update
  7.3 0.0 copy-start
  7.3 0.0 all-gather.6.cloned.1.call-start
  7.3 211.9 %all-gather.4.cloned.1.call-done = bf16[1,1536,12288]{2,1,0:T(8,128)(2,1)} async-done(((bf16[1,96,12288]{2,1,0:T(8,128)(2,1)}), bf16[1,1536,12288]{2,1,0:T(8,128)(2,1)}) %all-gather.4.cloned.1.call-update) | async-done | bytes 37748752 | tf_op jit(solution)/shard_map/all_gather | solution.py:17
  219.2 18.5 %fusion.19 = bf16[96,1536]{1,0:T(8,128)(2,1)} fusion(bf16[1,1536,12288]{2,1,0:T(8,128)(2,1)} %all-gather.4.cloned.1.call-done, bf16[1,96,12288]{2,1,0:T(8,128)(2,1)} %param.1), kind=kOutput, calls=%fused_computation.13 | convolution fusion | flops 3624026112 | bytes 40402944 | tf_op jit(solution)/shard_map/lrc,lkc->lrk/dot_general | solution.py:19
  237.7 0.0 all-gather.6.cloned.1.call-update
  237.8 55.6 %all-gather.6.cloned.1.call-done = bf16[1536,1536]{1,0:T(8,128)(2,1)} async-done(((bf16[96,1536]{1,0:T(8,128)(2,1)}), bf16[1536,1536]{1,0:T(8,128)(2,1)}) %all-gather.6.cloned.1.call-update) | async-done | bytes 4718608 | tf_op jit(solution)/shard_map/all_gather | solution.py:26
  293.3 0.0 copy-done
  293.3 22.3 %fusion.13 = bf16[1,96,12288]{2,1,0:T(8,128)(2,1)} fusion(bf16[1,1536,12288]{2,1,0:T(8,128)(2,1)} %all-gather.4.cloned.1.call-done, bf16[1,96,12288]{2,1,0:T(8,128)(2,1)S(1)} %copy-done, bf16[96,1536]{1,0:T(8,128)(2,1)} %fusion.19, bf16[1536,1536]{1,0:T(8,128)(2,1)} %all-gather.6.cloned.1.call-done), kind=kOutput, calls=%fused_computation.7 | convolution fusion | flops 4083499008 | bytes 47480832 | tf_op jit(solution)/shard_map/lrk,lkc->lrc/dot_general | solution.py:30
  315.6 13.5 %copy.5 = bf16[1,96,12288]{1,0,2:T(2,128)(2,1)} copy(bf16[1,96,12288]{2,1,0:T(8,128)(2,1)} %fusion.13) | data formatting | bytes 4718592 | tf_op jit(solution)/shard_map/convert_element_type | solution.py:33
  329.1 0.5 broadcast.2
  329.7 67.2 %reduce = bf16[12288,96]{1,0:T(8,128)(2,1)S(1)} reduce(bf16[12288,1,96]{2,1,0:T(2,128)(2,1)} %bitcast.42, bf16[]{:T(256)} %broadcast.2), dimensions={1}, to_apply=%bitcast.37.reduce_sub_computation | reduce | bytes 4718594
  396.8 6.0 %reshape.28 = bf16[8,2,73728]{2,1,0:T(2,128)(2,1)} reshape(bf16[12288,96]{1,0:T(8,128)(2,1)S(1)} %reduce) | data formatting | bytes 4718592
  402.8 34.6 %all_to_all.18 = bf16[8,2,73728]{2,1,0:T(2,128)(2,1)S(1)} all-to-all(bf16[8,2,73728]{2,1,0:T(2,128)(2,1)} %reshape.28), channel_id=1, replica_groups=mesh['layer'=8,'blk'=16] {'layer'}, dimensions={0} | all-to-all | bytes 4718592 | tf_op jit(solution)/shard_map/all_to_all | solution.py:34
  437.4 6.1 %reshape.29 = bf16[12288,1,96]{2,1,0:T(2,128)(2,1)} reshape(bf16[8,2,73728]{2,1,0:T(2,128)(2,1)S(1)} %all_to_all.18) | data formatting | bytes 4718592
  443.5 12.1 %copy.6 = bf16[1,96,12288]{2,1,0:T(8,128)(2,1)S(1)} copy(bf16[1,96,12288]{1,0,2:T(2,128)(2,1)} %bitcast.43) | data formatting | bytes 4718592 | tf_op jit(solution)/shard_map/all_to_all | solution.py:34
  455.6 0.8 copy.8
  456.4 0.2 bitcast_bitcast_fusion
  456.5 2.1 copy.7
Async XLA Ops:
  6.5 212.7 %all-gather.4.cloned.1.call-start = ((), (), s32[]{:S(2)}) async-start(), calls=%async_computation.1 | async-start | bytes 40108032 | tf_op jit(solution)/shard_map/all_gather | solution.py:17
  7.3 286.1 %copy-start = (bf16[1,96,12288]{2,1,0:T(8,128)(2,1)S(1)}, bf16[1,96,12288]{2,1,0:T(8,128)(2,1)}, u32[]{:S(2)}) copy-start(bf16[1,96,12288]{2,1,0:T(8,128)(2,1)} %param.1) | copy-start | bytes 7077892
  7.3 286.1 %all-gather.6.cloned.1.call-start = ((), (), s32[]{:S(2)}) async-start(), calls=%async_computation.2 | async-start | bytes 5013504 | tf_op jit(solution)/shard_map/all_gather | solution.py:26
Sparse Core Ops, SparseCore 0:
  9.8 209.4 all-gather.3
  237.9 55.3 all-gather.5
where the time goes:
time: 466 us; the launch traced here: 465 us
  waiting for transfers between devices  268 us (58%)
  other arithmetic  67.2 us (14%)
  local copies, waits for them, and re-layouts  41.2 us (9%)
  matrix products  40.8 us (9%)
  blocking collectives  34.6 us (7%)
  between operations  13.4 us (3%)
    all_gather x1, waiting for transfers between devices, shards(): pieces = lax.all_gather(iterate, 'blk', axis=1, tiled=True)  212 us
    unnamed x1, other arithmetic  67.2 us
    all_gather x1, waiting for transfers between devices, shards(): lax.all_gather(gram_half, 'blk', axis=1, tiled=True)  55.6 us
    all_to_all x1, blocking collectives, shards(): lax.all_to_all(scaled_rows, 'layer', split_axis=2, concat_axis=0, tiled=T...  34.6 us
    dot_general x1, matrix products, shards(): jnp.einsum('lrk,lkc->lrc', mixing, gathered, preferred_element_type=jnp.f...  22.3 us
    dot_general x1, matrix products, shards(): jnp.einsum('lrc,lkc->lrk', iterate, pieces, preferred_element_type=jnp.fl...  18.5 us
    all_to_all x3, local copies, waits for them, and re-layouts, shards(): lax.all_to_all(scaled_rows, 'layer', split_axis=2, concat_axis=0, tiled=T...  14.3 us
    convert_element_type x1, local copies, waits for them, and re-layouts, shards(): scaled_rows = (scale * result).astype(jnp.bfloat16)  13.5 us
  transfers between devices with their start and end apart: 2, of which 2 were waited for; matrix products, arithmetic and copies ran while one was open for 0% of the time, Pallas kernels for 0%

commit v1 on v0

--- a/solution.py
+++ b/solution.py
@@ -3,6 +3,7 @@
 import jax.numpy as jnp
 from jax import lax
 from jax.sharding import PartitionSpec as P
+from jax.lax import all_to_all, axis_size
 
 coeff_a = 3.4445
 coeff_b = -4.775
@@ -10,6 +11,12 @@
 
 
 def shards(iterate):
+
+    def search_frames_over_axis(m, array_dim, axis_no):
+        local_part = jnp.stack(jnp.split(m, axis_size("layer"), axis=array_dim))
+        opened = all_to_all(local_part, concat_axis=0, split_axis=0, axis_name="layer")
+        return jnp.concatenate(opened, axis=axis_no)
+
     local_rows = iterate.shape[1]
     width = iterate.shape[2]
     all_rows = local_rows * lax.axis_size("blk")
@@ -31,7 +38,7 @@
         "lrk,lkc->lrc", mixing, gathered, preferred_element_type=jnp.float32
     )
     scaled_rows = (scale * result).astype(jnp.bfloat16)
-    return lax.all_to_all(scaled_rows, "layer", split_axis=2, concat_axis=0, tiled=True)
+    return search_frames_over_axis(scaled_rows, 2, 0)
 
 
 def solution(mesh):

time: 466 us -> 366 us (0.79)
  other arithmetic: 67.2 us -> 0 us
  local copies, waits for them, and re-layouts: 41.2 us -> 9.28 us
    unnamed x1 -> x0, other arithmetic: 67.2 us -> none
    all_to_all x3 -> x0, local copies, waits for them, and re-layouts: 14.3 us -> none  [shards(): lax.all_to_all(scaled_rows, 'layer', split_axis=2, concat_axis=0, tiled=T...]
    convert_element_type x1 -> x0, local copies, waits for them, and re-layouts: 13.5 us -> none  [shards(): scaled_rows = (scale * result).astype(jnp.bfloat16)]
    unnamed x6 -> x10, local copies, waits for them, and re-layouts: 13.4 us -> 8.3 us
where the time goes in v1:
time: 366 us
  waiting for transfers between devices  268 us (73%)
  matrix products  40.2 us (11%)
  blocking collectives  34.4 us (9%)
  between operations  13.4 us (4%)
  local copies, waits for them, and re-layouts  9.28 us (3%)
    all_gather x1, waiting for transfers between devices, shards(): pieces = lax.all_gather(iterate, 'blk', axis=1, tiled=True)  212 us
    all_gather x1, waiting for transfers between devices, shards(): lax.all_gather(gram_half, 'blk', axis=1, tiled=True)  55.6 us
    all_to_all x1, blocking collectives, search_frames_over_axis(): all_to_all(local_part, concat_axis=0, split_axis=0, axis_name='layer')  34.4 us
    dot_general x1, matrix products, shards(): jnp.einsum('lrk,lkc->lrc', mixing, gathered, preferred_element_type=jnp.f...  22.3 us
    dot_general x1, matrix products, shards(): jnp.einsum('lrc,lkc->lrk', iterate, pieces, preferred_element_type=jnp.fl...  17.8 us
    unnamed x10, local copies, waits for them, and re-layouts  8.3 us
  transfers between devices with their start and end apart: 2, of which 2 were waited for; matrix products, arithmetic and copies ran while one was open for 0% of the time, Pallas kernels for 0%

profile of v1, /device:TPU:0, one launch (start us, length us, event | category | flops | bytes accessed | tf_op | source)
XLA Modules:
  0.0 365.6 jit_solution(12927268568163251979)
XLA Ops:
  6.5 0.0 copy-start
  6.5 0.0 all-gather.4.cloned.1.call-start
  6.5 0.7 all-gather.4.cloned.1.call-update
  7.3 0.0 all-gather.6.cloned.1.call-start
  7.3 211.9 %all-gather.4.cloned.1.call-done = bf16[1,1536,12288]{2,1,0:T(8,128)(2,1)} async-done(((bf16[1,96,12288]{2,1,0:T(8,128)(2,1)}), bf16[1,1536,12288]{2,1,0:T(8,128)(2,1)}) %all-gather.4.cloned.1.call-update) | async-done | bytes 37748752 | tf_op jit(solution)/shard_map/all_gather | solution.py:24
  219.2 0.0 copy-done
  219.2 17.8 %fusion.19 = bf16[96,1536]{1,0:T(8,128)(2,1)} fusion(bf16[1,1536,12288]{2,1,0:T(8,128)(2,1)} %all-gather.4.cloned.1.call-done, bf16[1,96,12288]{2,1,0:T(8,128)(2,1)S(1)} %copy-done), kind=kOutput, calls=%fused_computation.12 | convolution fusion | flops 3624026112 | bytes 40402944 | tf_op jit(solution)/shard_map/lrc,lkc->lrk/dot_general | solution.py:26
  237.1 0.0 all-gather.6.cloned.1.call-update
  237.1 55.6 %all-gather.6.cloned.1.call-done = bf16[1536,1536]{1,0:T(8,128)(2,1)} async-done(((bf16[96,1536]{1,0:T(8,128)(2,1)}), bf16[1536,1536]{1,0:T(8,128)(2,1)}) %all-gather.6.cloned.1.call-update) | async-done | bytes 4718608 | tf_op jit(solution)/shard_map/all_gather | solution.py:33
  292.7 22.3 %fusion.13 = bf16[1,96,12288]{2,1,0:T(8,128)(2,1)} fusion(bf16[1,1536,12288]{2,1,0:T(8,128)(2,1)} %all-gather.4.cloned.1.call-done, bf16[1,96,12288]{2,1,0:T(8,128)(2,1)S(1)} %copy-done, bf16[96,1536]{1,0:T(8,128)(2,1)} %fusion.19, bf16[1536,1536]{1,0:T(8,128)(2,1)} %all-gather.6.cloned.1.call-done), kind=kOutput, calls=%fused_computation.7 | convolution fusion | flops 4083499008 | bytes 47480832 | tf_op jit(solution)/shard_map/lrk,lkc->lrc/dot_general | solution.py:37
  315.0 1.0 fusion.33
  316.0 1.0 fusion.32
  317.0 1.0 fusion.31
  318.0 1.0 fusion.30
  319.0 1.0 fusion.29
  319.9 1.0 fusion.28
  320.9 1.0 fusion.27
  321.9 1.0 fusion.26
  322.9 34.4 %all_to_all.5 = bf16[8,1,96,1536]{3,2,1,0:T(8,128)(2,1)S(1)} all-to-all(bf16[8,1,96,1536]{3,2,1,0:T(8,128)(2,1)S(1)} %fusion.26), channel_id=1, replica_groups=mesh['layer'=8,'blk'=16] {'layer'}, dimensions={0} | all-to-all | bytes 4718592 | tf_op jit(solution)/shard_map/all_to_all | solution.py:17
  357.3 1.4 copy.10
Async XLA Ops:
  6.5 212.7 %copy-start = (bf16[1,96,12288]{2,1,0:T(8,128)(2,1)S(1)}, bf16[1,96,12288]{2,1,0:T(8,128)(2,1)}, u32[]{:S(2)}) copy-start(bf16[1,96,12288]{2,1,0:T(8,128)(2,1)} %param.1) | copy-start | bytes 7077892
  6.5 212.7 %all-gather.4.cloned.1.call-start = ((), (), s32[]{:S(2)}) async-start(), calls=%async_computation.1 | async-start | bytes 40108032 | tf_op jit(solution)/shard_map/all_gather | solution.py:24
  7.3 285.4 %all-gather.6.cloned.1.call-start = ((), (), s32[]{:S(2)}) async-start(), calls=%async_computation.2 | async-start | bytes 5013504 | tf_op jit(solution)/shard_map/all_gather | solution.py:33
Sparse Core Ops, SparseCore 0:
  9.8 209.4 all-gather.3
  237.2 55.3 all-gather.5

commit v2 on v0

--- a/solution.py
+++ b/solution.py
@@ -1,3 +1,4 @@
+import functools
 import math
 import jax
 import jax.numpy as jnp
@@ -9,12 +10,27 @@
 coeff_c = 2.0315
 
 
+def define_fields_by_axis(slab_in, net_axis):
+    return jnp.concatenate(
+        jax.lax.all_to_all(
+            jnp.stack([slab_in for _ in range(jax.lax.axis_size(net_axis))], 0),
+            axis_name=net_axis,
+            split_axis=0,
+            concat_axis=0,
+        ),
+        1,
+    )
+
+
+map_hubs = functools.partial(define_fields_by_axis, net_axis="blk")
+
+
 def shards(iterate):
     local_rows = iterate.shape[1]
     width = iterate.shape[2]
     all_rows = local_rows * lax.axis_size("blk")
     scale = math.sqrt(max(all_rows, width))
-    pieces = lax.all_gather(iterate, "blk", axis=1, tiled=True)
+    pieces = map_hubs(iterate)
     gathered = pieces
     gram_tile = jnp.einsum("lrc,lkc->lrk", iterate, pieces, preferred_element_type=jnp.float32)
     gram_block = gram_tile

time: 466 us -> 687 us (1.47)
  blocking collectives: 34.6 us -> 454 us
  waiting for transfers between devices: 268 us -> 56.8 us
  local copies, waits for them, and re-layouts: 41.2 us -> 54.8 us
    all_to_all x0 -> x1, blocking collectives: none -> 420 us  [define_fields_by_axis(): jax.lax.all_to_all(jnp.stack([slab_in for _ in range(jax.lax.axis_size(ne...]
    all_gather x1 -> x0, waiting for transfers between devices: 212 us -> none  [shards(): pieces = lax.all_gather(iterate, 'blk', axis=1, tiled=True)]
    another operation x0 -> x1, local copies, waits for them, and re-layouts: none -> 13.6 us  [define_fields_by_axis(): jnp.stack([slab_in for _ in range(jax.lax.axis_size(net_axis))], 0)]
  transfers between devices with their start and end apart: 2 -> 1, of which waited for: 2 -> 1; matrix products, arithmetic and copies ran while one was open for 0% -> 0% of each run, Pallas kernels for 0% -> 0%
where the time goes in v2:
time: 687 us; the launch traced here: 686 us
  blocking collectives  454 us (66%)
  other arithmetic  67.2 us (10%)
  waiting for transfers between devices  56.8 us (8%)
  local copies, waits for them, and re-layouts  54.8 us (8%)
  matrix products  40.1 us (6%)
  between operations  13.4 us (2%)
    all_to_all x1, blocking collectives, define_fields_by_axis(): jax.lax.all_to_all(jnp.stack([slab_in for _ in range(jax.lax.axis_size(ne...  420 us
    unnamed x1, other arithmetic  67.2 us
    all_gather x1, waiting for transfers between devices, shards(): lax.all_gather(gram_half, 'blk', axis=1, tiled=True)  56.8 us
    all_to_all x1, blocking collectives, shards(): lax.all_to_all(scaled_rows, 'layer', split_axis=2, concat_axis=0, tiled=T...  34.6 us
    dot_general x1, matrix products, shards(): jnp.einsum('lrk,lkc->lrc', mixing, gathered, preferred_element_type=jnp.f...  22.3 us
    dot_general x1, matrix products, shards(): jnp.einsum('lrc,lkc->lrk', iterate, pieces, preferred_element_type=jnp.fl...  17.8 us
    all_to_all x3, local copies, waits for them, and re-layouts, shards(): lax.all_to_all(scaled_rows, 'layer', split_axis=2, concat_axis=0, tiled=T...  14.3 us
  transfers between devices with their start and end apart: 1, of which 1 were waited for; matrix products, arithmetic and copies ran while one was open for 0% of the time, Pallas kernels for 0%

profile of v2, /device:TPU:0, one launch (start us, length us, event | category | flops | bytes accessed | tf_op | source)
XLA Modules:
  0.0 686.4 jit_solution(1221242351155050314)
XLA Ops:
  6.5 0.0 all-gather.3.cloned.1.call-start
  6.5 13.6 %stack.2 = bf16[16,1,96,12288]{3,2,1,0:T(8,128)(2,1)} broadcast(bf16[96,12288]{1,0:T(8,128)(2,1)} %bitcast.32), dimensions={2,3} | broadcast | bytes 40108032 | tf_op jit(solution)/shard_map/stack | solution.py:16
  20.1 0.0 copy-start
  20.1 419.6 %all_to_all.23 = bf16[16,1,96,12288]{3,2,1,0:T(8,128)(2,1)} all-to-all(bf16[16,1,96,12288]{3,2,1,0:T(8,128)(2,1)} %stack.2), channel_id=1, replica_groups=mesh['layer'=8,'blk'=16] {'blk'}, dimensions={0} | all-to-all | bytes 75497472 | tf_op jit(solution)/shard_map/all_to_all | solution.py:15
  439.7 0.0 copy-done
  439.7 17.8 %convolution_convert_fusion = bf16[96,1536]{1,0:T(8,128)(2,1)} fusion(bf16[1536,12288]{1,0:T(8,128)(2,1)} %bitcast.28, bf16[1,96,12288]{2,1,0:T(8,128)(2,1)S(1)} %copy-done), kind=kOutput, calls=%fused_computation.8 | convolution fusion | flops 3624026112 | bytes 40402944 | tf_op jit(solution)/shard_map/lrc,lkc->lrk/dot_general | solution.py:35
  457.5 0.0 all-gather.3.cloned.1.call-update
  457.5 56.8 %all-gather.3.cloned.1.call-done = bf16[1536,1536]{1,0:T(8,128)(2,1)} async-done(((bf16[96,1536]{1,0:T(8,128)(2,1)}), bf16[1536,1536]{1,0:T(8,128)(2,1)}) %all-gather.3.cloned.1.call-update) | async-done | bytes 4718608 | tf_op jit(solution)/shard_map/all_gather | solution.py:42
  514.3 22.3 %fusion.2 = bf16[1,96,12288]{2,1,0:T(8,128)(2,1)} fusion(bf16[1536,12288]{1,0:T(8,128)(2,1)} %bitcast.29, bf16[1,96,12288]{2,1,0:T(8,128)(2,1)S(1)} %copy-done, bf16[96,1536]{1,0:T(8,128)(2,1)} %convolution_convert_fusion, bf16[1536,1536]{1,0:T(8,128)(2,1)} %all-gather.3.cloned.1.call-done), kind=kOutput, calls=%fused_computation.3 | convolution fusion | flops 4083499008 | bytes 47480832 | tf_op jit(solution)/shard_map/lrk,lkc->lrc/dot_general | solution.py:46
  536.6 13.5 %copy.5 = bf16[1,96,12288]{1,0,2:T(2,128)(2,1)} copy(bf16[1,96,12288]{2,1,0:T(8,128)(2,1)} %fusion.2) | data formatting | bytes 4718592 | tf_op jit(solution)/shard_map/convert_element_type | solution.py:49
  550.1 0.5 broadcast.5
  550.6 67.2 %reduce = bf16[12288,96]{1,0:T(8,128)(2,1)S(1)} reduce(bf16[12288,1,96]{2,1,0:T(2,128)(2,1)} %bitcast.30, bf16[]{:T(256)} %broadcast.5), dimensions={1}, to_apply=%bitcast.21.reduce_sub_computation | reduce | bytes 4718594
  617.8 6.0 reshape.34
  623.8 34.6 %all_to_all.24 = bf16[8,2,73728]{2,1,0:T(2,128)(2,1)S(1)} all-to-all(bf16[8,2,73728]{2,1,0:T(2,128)(2,1)} %reshape.34), channel_id=1, replica_groups=mesh['layer'=8,'blk'=16] {'layer'}, dimensions={0} | all-to-all | bytes 4718592 | tf_op jit(solution)/shard_map/all_to_all | solution.py:50
  658.4 6.0 reshape.35
  664.5 12.1 %copy.6 = bf16[1,96,12288]{2,1,0:T(8,128)(2,1)S(1)} copy(bf16[1,96,12288]{1,0,2:T(2,128)(2,1)} %bitcast.31) | data formatting | bytes 4718592 | tf_op jit(solution)/shard_map/all_to_all | solution.py:50
  676.5 0.8 copy.8
  677.3 0.2 bitcast_bitcast_fusion
  677.5 2.1 copy.7
Async XLA Ops:
  6.5 507.8 %all-gather.3.cloned.1.call-start = ((), (), s32[]{:S(2)}) async-start(), calls=%async_computation.2 | async-start | bytes 5013504 | tf_op jit(solution)/shard_map/all_gather | solution.py:42
  20.1 419.6 %copy-start = (bf16[1,96,12288]{2,1,0:T(8,128)(2,1)S(1)}, bf16[1,96,12288]{2,1,0:T(8,128)(2,1)}, u32[]{:S(2)}) copy-start(bf16[1,96,12288]{2,1,0:T(8,128)(2,1)} %param.1) | copy-start | bytes 7077892
Sparse Core Ops, SparseCore 0:
  457.6 56.6 all-gather.2
